TPU v7x, 32 devices: a whole 2x2x4 slice. The times are simulated.
32 devices in a mesh: wide: 8 (over y, x, core), blk: 4 (over z).
Axes of the slice: x: 2, y: 2, z: 4, core: 2. Of those that a mesh axis runs over, the one named last changes fastest.
Arguments:
- audio: bfloat16 [4096, 1024], P(('wide', 'blk')), may hold values from -1 to 1
- video: bfloat16 [4096, 1024], P(('wide', 'blk')), may hold values from -1 to 1
- owner: int32 [4096, 1], P(('wide', 'blk')), may hold values from 0 to 7; in each aligned block of 128 rows (0 to 127, 128 to 255, ...) at most 32 rows name the same one
- clip_feats: bfloat16 [8192, 1024], P(('wide', 'blk')), may hold values from -24 to 24
- lengths: int32 [8192], P(('wide', 'blk')), may hold values from 1 to 16
- proj_weight: bfloat16 [1024, 1024], replicated, may hold values from -0.1875 to 0.1875
Outputs:
- audio_grad: bfloat16 [4096, 1024], P(('wide', 'blk'))
- feats_grad: bfloat16 [8192, 1024], P(('wide', 'blk'))
- weight_grad: float32 [1024, 1024], P('wide')
Inputs may be any that keep to these rules, and one draw needn't show every extreme that they name: Among the 128 rows of one device, no owner is named more than 32 times, a bound that some block reaches.
All inputs are finite; a program needn't handle non-finite values.
Results may differ from a plain program's by a relative error of at most 0.02.
Values may be sent and summed in bfloat16 or wider, within the bound.
A program may use at most 64 MiB of HBM per device.

v0:
```python
from functools import partial

import jax
import jax.numpy as jnp
from jax import lax
from jax.sharding import PartitionSpec as P


def rows_dot(matrix_a, matrix_b):
    return lax.dot_general(
        matrix_a, matrix_b, (((1,), (1,)), ((), ())), preferred_element_type=jnp.float32
    )


def cols_dot(matrix_a, matrix_b):
    return lax.dot_general(
        matrix_a, matrix_b, (((0,), (0,)), ((), ())), preferred_element_type=jnp.float32
    )


def pair_coeffs(scores, labels, factor):
    return (factor * (jax.nn.sigmoid(4.0 * scores - 2.0) - labels)).astype(jnp.bfloat16)


def shards(audio, video, owner, clip_feats, lengths, proj_weight):
    blocks = lax.axis_size("blk")
    clip_count = audio.shape[0]
    feature_count = audio.shape[1]
    factor = 4.0 / blocks
    row_ids = jnp.arange(clip_count, dtype=jnp.int32)
    offset = lax.axis_index("blk") * clip_count
    gathered = lax.all_gather(video, "blk", axis=0, tiled=True)
    other_ids = jnp.arange(gathered.shape[0], dtype=jnp.int32)
    labels = ((offset + row_ids)[:, None] == other_ids[None, :]).astype(jnp.float32)
    coeffs = pair_coeffs(rows_dot(audio, gathered), labels, factor)
    audio_total = jnp.dot(coeffs, gathered, preferred_element_type=jnp.float32)
    gathered = lax.all_gather(audio, "blk", axis=0, tiled=True)
    other_ids = jnp.arange(gathered.shape[0], dtype=jnp.int32)
    labels = (other_ids[:, None] == (offset + row_ids)[None, :]).astype(jnp.float32)
    coeffs = pair_coeffs(rows_dot(gathered, video), labels, factor)
    video_sum = cols_dot(coeffs, gathered)
    audio_grad = audio_total.astype(jnp.bfloat16)
    video_grad = video_sum.astype(jnp.bfloat16)
    peer_count = lax.axis_size("wide")
    slot_count = clip_feats.shape[0]
    capacity = slot_count // peer_count
    owner_peer = owner[:, 0]
    onehot = (owner_peer[:, None] == jnp.arange(peer_count, dtype=jnp.int32)[None, :]).astype(
        jnp.int32
    )
    slot_rank = jnp.sum((jnp.cumsum(onehot, axis=0) - onehot) * onehot, axis=1)
    target = owner_peer * capacity + slot_rank
    placing = (jnp.arange(slot_count, dtype=jnp.int32)[:, None] == target[None, :]).astype(
        jnp.bfloat16
    )
    packed = jnp.dot(placing, video_grad, preferred_element_type=jnp.float32).astype(jnp.bfloat16)
    packed = packed.reshape(peer_count, capacity, feature_count)
    received = lax.all_to_all(packed, "wide", split_axis=0, concat_axis=0, tiled=True).reshape(
        slot_count, feature_count
    )
    length_scale = lax.rsqrt(lengths.astype(jnp.float32))[:, None]
    pooled = (clip_feats.astype(jnp.float32) * length_scale).astype(jnp.bfloat16)
    preact = jnp.dot(pooled, proj_weight, preferred_element_type=jnp.float32)
    _, pullback = jax.vjp(partial(jax.nn.gelu, approximate=False), preact)
    pre_grad = pullback(received.astype(jnp.float32))[0].astype(jnp.bfloat16)
    feats_grad = (rows_dot(pre_grad, proj_weight) * length_scale).astype(jnp.bfloat16)
    partial_rows = lax.psum_scatter(
        cols_dot(pooled, pre_grad).astype(jnp.bfloat16), "wide", scatter_dimension=0, tiled=True
    )
    weight_grad = lax.psum(partial_rows, "blk").astype(jnp.float32)
    return (audio_grad, feats_grad, weight_grad)


def solution(mesh):
    return jax.shard_map(
        shards,
        mesh=mesh,
        in_specs=(
            P(("wide", "blk"), None),
            P(("wide", "blk"), None),
            P(("wide", "blk"), None),
            P(("wide", "blk"), None),
            P(("wide", "blk")),
            P(),
        ),
        out_specs=(P(("wide", "blk"), None), P(("wide", "blk"), None), P("wide", None)),
        check_vma=False,
    )
```

profile of v0, /device:TPU:0, one launch (start us, length us, event | category | flops | bytes accessed | tf_op | source)
XLA Modules:
  0.0 167.4 jit_solution(1915806834253951210)
XLA Ops:
  7.2 0.0 copy-start
  7.2 0.0 all-gather.5.cloned.1.call-start
  7.2 0.7 all-gather.5.cloned.1.call-update
  7.9 0.7 fusion.37
  8.7 0.2 reduce_window_sum.11
  8.8 0.8 select_reduce_fusion
  9.7 0.7 multiply_add_fusion
  10.3 30.0 %all-gather.5.cloned.1.call-done = bf16[512,1024]{1,0:T(8,128)(2,1)} async-done(((bf16[128,1024]{1,0:T(8,128)(2,1)}), bf16[512,1024]{1,0:T(8,128)(2,1)}) %all-gather.5.cloned.1.call-update) | async-done | bytes 1048592 | tf_op jit(solution)/shard_map/all_gather | solution.py:37
  40.3 1.8 %fusion.14 = bf16[512,128]{1,0:T(8,128)(2,1)S(1)} fusion(bf16[512,1024]{1,0:T(8,128)(2,1)} %all-gather.5.cloned.1.call-done, bf16[128,1024]{1,0:T(8,128)(2,1)} %param.7, s32[128]{0:T(128)S(1)} %iota_add_fusion), kind=kOutput, calls=%fused_computation.24 | convolution fusion | flops 134807552 | bytes 1442304 | tf_op jit(solution)/shard_map/dot_general | solution.py:10
  42.1 0.0 copy-start.6
  42.1 1.4 convolution_convert_fusion.1
  43.5 3.7 %all-to-all-start = ((bf16[8,32,1024]{2,1,0:T(8,128)(2,1)}), bf16[8,32,1024]{2,1,0:T(8,128)(2,1)S(1)}, u32[]{:S(2)}, u32[]{:S(2)}) async-start(bf16[8,32,1024]{2,1,0:T(8,128)(2,1)} %bitcast.1), calls=%async_computation | async-start | bytes 1048576 | tf_op jit(solution)/shard_map/all_to_all | solution.py:58
  47.2 0.0 all-gather.3.cloned.1.call-start
  47.2 0.7 all-gather.3.cloned.1.call-update
  47.9 0.0 reduce-scatter.2.cloned.1.call-start
  48.0 0.0 copy-start.2
  48.0 8.9 %all-to-all-done = bf16[8,32,1024]{2,1,0:T(8,128)(2,1)S(1)} async-done(((bf16[8,32,1024]{2,1,0:T(8,128)(2,1)}), bf16[8,32,1024]{2,1,0:T(8,128)(2,1)S(1)}, u32[]{:S(2)}, u32[]{:S(2)}) %all-to-all-start) | async-done | bytes 524320 | tf_op jit(solution)/shard_map/all_to_all | solution.py:58
  56.9 4.2 %fusion.20 = bf16[256,1024]{1,0:T(8,128)(2,1)S(1)} fusion(bf16[8,32,1024]{2,1,0:T(8,128)(2,1)S(1)} %all-to-all-done, bf16[1024,1024]{1,0:T(8,128)(2,1)S(1)} %copy-done, bf16[256,1024]{1,0:T(8,128)(2,1)} %param.9, f32[256]{0:T(256)S(1)} %convert_rsqrt_fusion), kind=kOutput, calls=%fused_computation.30 | convolution fusion | flops 556793856 | bytes 3671040 | tf_op jit(solution)/shard_map/dot_general | solution.py:63
  61.1 0.0 copy-start.3
  61.1 0.8 copy-done.3
  61.9 2.2 %convolution_convert_fusion = bf16[1024,1024]{1,0:T(8,128)(2,1)} fusion(bf16[256,1024]{1,0:T(8,128)(2,1)S(1)} %fusion.20, bf16[256,1024]{1,0:T(8,128)(2,1)S(1)} %copy-done.2, f32[256]{0:T(256)S(1)} %convert_rsqrt_fusion), kind=kOutput, calls=%fused_computation | convolution fusion | flops 538705920 | bytes 3146752 | tf_op jit(solution)/shard_map/dot_general | solution.py:16
  64.1 0.0 reduce-scatter.2.cloned.1.call-update
  64.1 0.0 copy-start.4
  64.1 0.0 all-reduce.2.cloned.1.call-start
  64.2 13.3 %all-gather.3.cloned.1.call-done = bf16[512,1024]{1,0:T(8,128)(2,1)} async-done(((bf16[128,1024]{1,0:T(8,128)(2,1)}), bf16[512,1024]{1,0:T(8,128)(2,1)}) %all-gather.3.cloned.1.call-update) | async-done | bytes 1048592 | tf_op jit(solution)/shard_map/all_gather | solution.py:32
  77.5 3.1 %convolution_convert_fusion.3 = bf16[128,1024]{1,0:T(8,128)(2,1)} fusion(bf16[512,1024]{1,0:T(8,128)(2,1)} %all-gather.3.cloned.1.call-done, bf16[128,1024]{1,0:T(8,128)(2,1)S(1)} %copy-done.5, s32[128]{0:T(128)S(1)} %iota_add_fusion), kind=kOutput, calls=%fused_computation.8 | convolution fusion | flops 269156352 | bytes 1573376 | tf_op jit(solution)/shard_map/dot_general | solution.py:36
  80.5 40.8 %reduce-scatter.2.cloned.1.call-done = bf16[128,1024]{1,0:T(8,128)(2,1)} async-done(((bf16[1024,1024]{1,0:T(8,128)(2,1)}), bf16[128,1024]{1,0:T(8,128)(2,1)}) %reduce-scatter.2.cloned.1.call-update) | async-done | bytes 262160 | tf_op jit(solution)/shard_map/reduce_scatter | solution.py:67
  121.3 0.0 all-reduce.2.cloned.1.call-update
  121.3 0.0 copy-done.4
  121.3 1.6 fusion
  122.9 36.2 %all-reduce.2.cloned.1.call-done = bf16[128,1024]{1,0:T(8,128)(2,1)} async-done(((bf16[128,1024]{1,0:T(8,128)(2,1)}), bf16[128,1024]{1,0:T(8,128)(2,1)}) %all-reduce.2.cloned.1.call-update) | async-done | bytes 262160 | tf_op jit(solution)/shard_map/psum | solution.py:70
  159.1 1.8 %convert_element_type.68 = f32[128,1024]{1,0:T(8,128)} convert(bf16[128,1024]{1,0:T(8,128)(2,1)} %all-reduce.2.cloned.1.call-done) | non-fusion elementwise | flops 131072 | bytes 786432 | tf_op jit(solution)/shard_map/convert_element_type | solution.py:70
  (9 shorter events, 0.0 us)
Async XLA Ops:
  7.2 49.7 %copy-start = (bf16[1024,1024]{1,0:T(8,128)(2,1)S(1)}, bf16[1024,1024]{1,0:T(8,128)(2,1)}, u32[]{:S(2)}) copy-start(bf16[1024,1024]{1,0:T(8,128)(2,1)} %param.11) | copy-start | bytes 6291460
  7.2 33.1 %all-gather.5.cloned.1.call-start = ((), (), s32[]{:S(2)}) async-start(), calls=%async_computation.3 | async-start | bytes 1310720 | tf_op jit(solution)/shard_map/all_gather | solution.py:37
  40.3 1.8 %copy-start.1 = (bf16[512,1024]{1,0:T(8,128)(2,1)S(1)}, bf16[512,1024]{1,0:T(8,128)(2,1)}, u32[]{:S(2)}) copy-start(bf16[512,1024]{1,0:T(8,128)(2,1)} %all-gather.5.cloned.1.call-done) | copy-start | bytes 3145732
  42.1 5.8 %copy-start.6 = (s32[256]{0:T(256)S(1)}, s32[256]{0:T(256)}, u32[]{:S(2)}) copy-start(s32[256]{0:T(256)} %param.10) | copy-start | bytes 3076
  43.5 13.4 %all-to-all-start = ((bf16[8,32,1024]{2,1,0:T(8,128)(2,1)}), bf16[8,32,1024]{2,1,0:T(8,128)(2,1)S(1)}, u32[]{:S(2)}, u32[]{:S(2)}) async-start(bf16[8,32,1024]{2,1,0:T(8,128)(2,1)} %bitcast.1), calls=%async_computation | async-start | bytes 1048576 | tf_op jit(solution)/shard_map/all_to_all | solution.py:58
  47.2 30.3 %all-gather.3.cloned.1.call-start = ((), (), s32[]{:S(2)}) async-start(), calls=%async_computation.2 | async-start | bytes 1310720 | tf_op jit(solution)/shard_map/all_gather | solution.py:32
  47.9 73.4 %reduce-scatter.2.cloned.1.call-start = ((), (), s32[]{:S(2)}) async-start(), calls=%async_computation.4 | async-start | bytes 2359296 | tf_op jit(solution)/shard_map/reduce_scatter | solution.py:67
  48.0 13.9 %copy-start.2 = (bf16[256,1024]{1,0:T(8,128)(2,1)S(1)}, bf16[256,1024]{1,0:T(8,128)(2,1)}, u32[]{:S(2)}) copy-start(bf16[256,1024]{1,0:T(8,128)(2,1)} %param.9) | copy-start | bytes 1572868
  61.1 0.8 copy-start.3
  61.9 15.6 %copy-start.5 = (bf16[128,1024]{1,0:T(8,128)(2,1)S(1)}, bf16[128,1024]{1,0:T(8,128)(2,1)}, u32[]{:S(2)}) copy-start(bf16[128,1024]{1,0:T(8,128)(2,1)} %param.6) | copy-start | bytes 786436
  64.1 57.2 %copy-start.4 = (bf16[256,1024]{1,0:T(8,128)(2,1)S(1)}, bf16[256,1024]{1,0:T(8,128)(2,1)}, u32[]{:S(2)}) copy-start(bf16[256,1024]{1,0:T(8,128)(2,1)} %copy-done.3) | copy-start | bytes 1572868
  64.1 95.0 %all-reduce.2.cloned.1.call-start = ((), (), s32[]{:S(2)}) async-start(), calls=%async_computation.5 | async-start | bytes 524288 | tf_op jit(solution)/shard_map/psum | solution.py:70
Sparse Core Ops, SparseCore 0:
  9.6 30.6 all-gather.4
  49.5 27.8 all-gather.2
  80.7 40.4 reduce-scatter.1
  123.5 35.5 all-reduce.1
where the time goes:
time: 168 us; the launch traced here: 167 us
  waiting for transfers between devices  131 us (78%)
  matrix products  14.2 us (8%)
  between operations  13.9 us (8%)
  other arithmetic  4.2 us (2%)
  starting transfers between devices  3.81 us (2%)
    reduce_scatter x1, waiting for transfers between devices, shards(): lax.psum_scatter(cols_dot(pooled, pre_grad).astype(jnp.bfloat16), 'wide',...  40.8 us
    psum x1, waiting for transfers between devices, shards(): weight_grad = lax.psum(partial_rows, 'blk').astype(jnp.float32)  36.2 us
    all_gather x1, waiting for transfers between devices, shards(): gathered = lax.all_gather(audio, 'blk', axis=0, tiled=True)  30 us
    all_gather x1, waiting for transfers between devices, shards(): gathered = lax.all_gather(video, 'blk', axis=0, tiled=True)  13.3 us
    all_to_all x1, waiting for transfers between devices, shards(): lax.all_to_all(packed, 'wide', split_axis=0, concat_axis=0, tiled=True)  8.88 us
    dot_general x1, matrix products, shards(): preact = jnp.dot(pooled, proj_weight, preferred_element_type=jnp.float32)  4.22 us
    all_to_all x1, starting transfers between devices, shards(): lax.all_to_all(packed, 'wide', split_axis=0, concat_axis=0, tiled=True)  3.65 us
    dot_general x2, matrix products, rows_dot(): lax.dot_general(matrix_a, matrix_b, (((1,), (1,)), ((), ())), preferred_e...  3.41 us
  transfers between devices with their start and end apart: 5, of which 5 were waited for; matrix products, arithmetic and copies ran while one was open for 8% of the time, Pallas kernels for 0%

commit v1 on v0

v1 whole, which is shorter than its diff:
```python
import functools

import jax
import jax.numpy as jnp
from jax import lax
from jax.experimental import pallas as pl
from jax.experimental.pallas import tpu as pltpu
from jax.sharding import PartitionSpec as P

F32 = jnp.float32
BF16 = jnp.bfloat16
TILE = 256
SPLIT = 2


def dot(a, b):
    return jnp.dot(a, b, preferred_element_type=F32)


def rows_dot(a, b):
    return lax.dot_general(a, b, (((1,), (1,)), ((), ())), preferred_element_type=F32)


def column_of(row):
    n = row.shape[1]
    diagonal = lax.broadcasted_iota(jnp.int32, (n, n), 0) == lax.broadcasted_iota(
        jnp.int32, (n, n), 1
    )
    return jnp.sum(jnp.where(diagonal, row, jnp.zeros_like(row)), axis=1, keepdims=True)


def kernel(
    nw, nb,
    audio, video, owner, lengths, feats_hbm, weight_hbm,
    audio_out, feats_out, weight_out,
    feats, weight, a_buf, v_buf, a_acc, v_acc, v_grad, scale, pooled, pooled_t, pooled_p,
    gate, packed, received, pre, pre_p, acc, snd, rcv, fin, zs, zr,
    local_sem, a_send, a_recv, v_send, v_recv, p_send, p_recv, x_send, x_recv,
    g_send, g_recv, r_send, r_recv, z_send, z_recv,
):
    w, k = lax.axis_index("wide"), lax.axis_index("blk")
    rows, width = audio.shape
    slots = feats.shape[0]
    cap = slots // nw
    block = width // nw
    half = width // 2
    n2 = nw // 2
    bits = n2.bit_length() - 1
    chunks, _, chunk = fin.shape
    per_half = chunks // 2
    factor = 4.0 / nb
    core = lax.rem(w, 2)
    partner = w + 1 - 2 * core
    mine = w // 2

    def remote(src, dst, send, recv, dw, dk):
        return pltpu.make_async_remote_copy(
            src_ref=src, dst_ref=dst, send_sem=send, recv_sem=recv,
            device_id=(dw, dk), device_id_type=pl.DeviceIdType.MESH,
        )

    w_copy = pltpu.make_async_copy(weight_hbm, weight, local_sem.at[0])
    f_copy = pltpu.make_async_copy(feats_hbm, feats, local_sem.at[1])
    f_copy.start()
    w_copy.start()

    barrier = pltpu.get_barrier_semaphore()

    def peer_of(d):
        return lax.rem(w + d, nw)

    @pl.loop(1, nw)
    def _(d):
        pl.semaphore_signal(
            barrier, inc=1, device_id=(peer_of(d), k), device_id_type=pl.DeviceIdType.MESH
        )

    @pl.when(k > 0)
    def _():
        pl.semaphore_signal(
            barrier, inc=1, device_id=(w, k - 1), device_id_type=pl.DeviceIdType.MESH
        )

    @pl.when(k < nb - 1)
    def _():
        pl.semaphore_signal(
            barrier, inc=1, device_id=(w, k + 1), device_id_type=pl.DeviceIdType.MESH
        )

    sides = jnp.where(k > 0, 1, 0) + jnp.where(k < nb - 1, 1, 0)
    pl.semaphore_wait(barrier, nw - 1 + sides)

    def hop(src, buf, send, recv, j, step):
        side = 0 if step > 0 else 1
        return remote(src, buf.at[j], send.at[side, j], recv.at[j], w, k + step)

    def forward(src, buf, send, recv, j, step):
        @pl.when((k < nb - 1) if step > 0 else (k > 0))
        def _():
            hop(src, buf, send, recv, j, step).start()

    def begin(own, buf, send, recv):
        forward(own, buf, send, recv, k, 1)
        forward(own, buf, send, recv, k, -1)

    def coeffs(scores, labels):
        return (factor * (jax.nn.sigmoid(4.0 * scores - 2.0) - labels)).astype(BF16)

    def add_block(own, other, total):
        total[...] += dot(coeffs(rows_dot(own[...], other[...]), 0.0), other[...])

    def relay(s, buf, send, recv, own, total):
        for step in (1, -1):
            j = k - step * s

            @pl.when((j >= 0) if step > 0 else (j <= nb - 1))
            def _():
                hop(buf.at[j], buf, send, recv, j, step).wait_recv()
                forward(buf.at[j], buf, send, recv, j, step)

        for step in (1, -1):
            j = k - step * s

            @pl.when((j >= 0) if step > 0 else (j <= nb - 1))
            def _():
                add_block(own, buf.at[j], total)

    def finish(own, buf, send, recv):
        for s in range(nb):
            for step in (1, -1):
                j = k - step * s

                @pl.when(
                    ((j >= 0) & (k < nb - 1)) if step > 0 else ((j <= nb - 1) & (k > 0))
                )
                def _():
                    hop(own if s == 0 else buf.at[j], buf, send, recv, j, step).wait_send()

    begin(audio, a_buf, a_send, a_recv)

    eye = (
        lax.broadcasted_iota(jnp.int32, (rows, rows), 0)
        == lax.broadcasted_iota(jnp.int32, (rows, rows), 1)
    ).astype(F32)
    v_acc[...] = dot(coeffs(rows_dot(video[...], audio[...]), eye), audio[...])
    a_acc[...] = dot(coeffs(rows_dot(audio[...], video[...]), eye), video[...])

    scale[...] = column_of(lax.rsqrt(lengths[...].astype(F32)))
    f_copy.wait()

    @pl.loop(0, width // TILE)
    def _(t):
        cols = pl.ds(pl.multiple_of(t * TILE, TILE), TILE)
        part = (feats[:, cols].astype(F32) * scale[...]).astype(BF16)
        pooled[:, cols] = part
        pooled_t[cols, :] = part.astype(F32).T.astype(BF16)

    def pooled_copy(i):
        other = 2 * i + 1 - core
        start = pl.multiple_of(other * block, block)
        return remote(
            pooled_t.at[pl.ds(start, block), :], pooled_p.at[i],
            p_send.at[i], p_recv.at[i], partner, k,
        )

    @pl.loop(0, n2)
    def _(i):
        pooled_copy(i).start()

    w_copy.wait()

    @pl.loop(0, width // TILE)
    def _(t):
        cols = pl.ds(pl.multiple_of(t * TILE, TILE), TILE)
        v = dot(pooled[...], weight[:, cols])
        cdf = 0.5 * (1.0 + lax.erf(v * (0.5**0.5)))
        density = jnp.exp(-0.5 * v * v) * 0.3989422804014327
        gate[:, cols] = cdf + v * density

    for s in range(1, nb):
        relay(s, a_buf, a_send, a_recv, video, v_acc)
        if s == max(1, nb - 2):
            begin(video, v_buf, v_send, v_recv)

    v_grad[...] = v_acc[...].astype(BF16)
    own_row = owner[...]
    own_col = column_of(own_row)
    earlier = lax.broadcasted_iota(jnp.int32, (rows, rows), 0) < lax.broadcasted_iota(
        jnp.int32, (rows, rows), 1
    )
    same = (own_col == own_row) & earlier
    rank = jnp.sum(jnp.where(same, 1, 0), axis=0, keepdims=True)
    target = own_row * cap + rank
    placing = (
        (lax.broadcasted_iota(jnp.int32, (slots, rows), 0) == target).astype(F32).astype(BF16)
    )
    for t in range(width // TILE):
        cols = slice(t * TILE, (t + 1) * TILE)
        placed = dot(placing, v_grad[:, cols])
        packed[:, :, cols] = placed.reshape(nw, cap, TILE).astype(BF16)

    def exchange(peer):
        return remote(
            packed.at[peer], received.at[w], x_send.at[peer], x_recv.at[w], peer, k
        )

    @pl.loop(1, nw)
    def _(d):
        exchange(peer_of(d)).start()

    received[w] = packed[w]

    relay(1, v_buf, v_send, v_recv, audio, a_acc)

    @pl.loop(1, nw)
    def _(d):
        peer = peer_of(d)
        remote(
            packed.at[peer], received.at[peer], x_send.at[peer], x_recv.at[peer], peer, k
        ).wait_recv()

    def grad_copy(h):
        return remote(pre.at[h], pre_p.at[h], g_send.at[h], g_recv.at[h], partner, k)

    for h in range(2):
        for t in range(half // TILE):
            lo = h * half + t * TILE
            cols = slice(lo, lo + TILE)
            grads = received[:, :, cols].astype(F32).reshape(slots, TILE)
            pre[h, :, t * TILE : (t + 1) * TILE] = (grads * gate[:, cols]).astype(BF16)
        grad_copy(h).start()

    @pl.loop(0, n2)
    def _(i):
        pooled_copy(i).wait_recv()

    def order(h):
        return list(range(bits)) if h == 0 else list(range(bits))[::-1]

    def index(h, t, flip, combo):
        taken = order(h)
        at = 0
        for place, bit in enumerate(taken):
            own = lax.rem(mine // (1 << bit), 2)
            if place < t:
                value = own
            elif place == t:
                value = 1 - own if flip else own
            else:
                value = (combo >> (place - t - 1)) & 1
            at = at + value * (1 << bit)
        return at

    def product(h, i):
        start = pl.multiple_of((2 * i + core) * block, block)
        return dot(pooled_t[pl.ds(start, block), :], pre[h]) + dot(pooled_p[i], pre_p[h])

    def scatter_copy(h, t, combo):
        bit = order(h)[t]
        sign = 1 - 2 * lax.rem(mine // (1 << bit), 2)
        peer = w + sign * (2 << bit)
        slot = n2 - (1 << (bits - t)) + combo
        return remote(
            snd.at[h, slot], rcv.at[h, slot], r_send.at[h, slot], r_recv.at[h, slot], peer, k
        )

    def combos(t):
        return range(1 << (bits - 1 - t))

    def slot_of(t, combo):
        return n2 - (1 << (bits - t)) + combo

    for h in range(2):
        grad_copy(h).wait_recv()
        for combo in combos(0):
            snd[h, slot_of(0, combo)] = product(h, index(h, 0, 1, combo)).astype(BF16)
            scatter_copy(h, 0, combo).start()
    for h in range(2):
        for combo in combos(0):
            i = index(h, 0, 0, combo)
            acc[h, i] = product(h, i)

    for s in range(2, nb - 1):
        relay(s, v_buf, v_send, v_recv, audio, a_acc)

    @pl.loop(0, width // TILE)
    def _(t):
        cols = pl.ds(pl.multiple_of(t * TILE, TILE), TILE)
        out = rows_dot(pre[0], weight[cols, :half]) + rows_dot(pre[1], weight[cols, half:])
        feats_out[:, cols] = (out * scale[...]).astype(BF16)

    for t in range(bits):
        for h in range(2):
            for combo in combos(t):
                scatter_copy(h, t, combo).wait_recv()
                i = index(h, t, 0, combo)
                acc[h, i] += rcv[h, slot_of(t, combo)].astype(F32)
            if t + 1 < bits:
                for combo in combos(t + 1):
                    i = index(h, t + 1, 1, combo)
                    snd[h, slot_of(t + 1, combo)] = acc[h, i].astype(BF16)
                    scatter_copy(h, t + 1, combo).start()

    for h in range(2):
        for q in range(per_half):
            fin[h * per_half + q] = acc[h, mine, :, q * chunk : (q + 1) * chunk]

    def sum_copy(side, q):
        return remote(
            zs.at[side, q], zr.at[side, q], z_send.at[side, q], z_recv.at[side, q],
            w, k + 1 - 2 * side,
        )

    @pl.loop(0, nb - 1 + chunks)
    def _(time):
        for side in range(2):
            place = k if side == 0 else nb - 1 - k
            q = time - place

            @pl.when((q >= 0) & (q < chunks))
            def _():
                @pl.when(place > 0)
                def _():
                    sum_copy(side, q).wait_recv()

                @pl.when(place < nb - 1)
                def _():
                    @pl.when(place > 0)
                    def _():
                        zs[side, q] = (fin[q] + zr[side, q].astype(F32)).astype(BF16)

                    @pl.when(place == 0)
                    def _():
                        zs[side, q] = fin[q].astype(BF16)

                    sum_copy(side, q).start()

    for q in range(chunks):
        cols = slice(q * chunk, (q + 1) * chunk)
        weight_out[:, cols] = fin[q]

        @pl.when(k > 0)
        def _():
            weight_out[:, cols] += zr[0, q].astype(F32)

        @pl.when(k < nb - 1)
        def _():
            weight_out[:, cols] += zr[1, q].astype(F32)

    for s in range(max(2, nb - 1), nb):
        relay(s, v_buf, v_send, v_recv, audio, a_acc)
    audio_out[...] = a_acc[...].astype(BF16)

    finish(audio, a_buf, a_send, a_recv)
    finish(video, v_buf, v_send, v_recv)

    @pl.loop(0, n2)
    def _(i):
        pooled_copy(i).wait_send()

    @pl.loop(1, nw)
    def _(d):
        exchange(peer_of(d)).wait_send()

    for h in range(2):
        grad_copy(h).wait_send()
        for t in range(bits):
            for combo in combos(t):
                scatter_copy(h, t, combo).wait_send()

    @pl.loop(0, chunks)
    def _(q):
        @pl.when(k < nb - 1)
        def _():
            sum_copy(0, q).wait_send()

        @pl.when(k > 0)
        def _():
            sum_copy(1, q).wait_send()


def shards(nw, nb, audio, video, owner, clip_feats, lengths, proj_weight):
    rows, width = audio.shape
    slots = clip_feats.shape[0]
    cap, block, half, n2 = slots // nw, width // nw, width // 2, nw // 2
    chunks = 2 * SPLIT
    chunk = width // chunks
    vmem = pl.BlockSpec(memory_space=pltpu.VMEM)
    hbm = pl.BlockSpec(memory_space=pl.ANY)
    dma = pltpu.SemaphoreType.DMA
    return pl.pallas_call(
        functools.partial(kernel, nw, nb),
        out_shape=(
            jax.ShapeDtypeStruct((rows, width), BF16),
            jax.ShapeDtypeStruct((slots, width), BF16),
            jax.ShapeDtypeStruct((block, width), F32),
        ),
        in_specs=[vmem, vmem, vmem, vmem, hbm, hbm],
        out_specs=(vmem, vmem, vmem),
        scratch_shapes=[
            pltpu.VMEM((slots, width), BF16),
            pltpu.VMEM(proj_weight.shape, BF16),
            pltpu.VMEM((nb, rows, width), BF16),
            pltpu.VMEM((nb, rows, width), BF16),
            pltpu.VMEM((rows, width), F32),
            pltpu.VMEM((rows, width), F32),
            pltpu.VMEM((rows, width), BF16),
            pltpu.VMEM((slots, 1), F32),
            pltpu.VMEM((slots, width), BF16),
            pltpu.VMEM((width, slots), BF16),
            pltpu.VMEM((n2, block, slots), BF16),
            pltpu.VMEM((slots, width), F32),
            pltpu.VMEM((nw, cap, width), BF16),
            pltpu.VMEM((nw, cap, width), BF16),
            pltpu.VMEM((2, slots, half), BF16),
            pltpu.VMEM((2, slots, half), BF16),
            pltpu.VMEM((2, n2, block, half), F32),
            pltpu.VMEM((2, n2, block, half), BF16),
            pltpu.VMEM((2, n2, block, half), BF16),
            pltpu.VMEM((chunks, block, chunk), F32),
            pltpu.VMEM((2, chunks, block, chunk), BF16),
            pltpu.VMEM((2, chunks, block, chunk), BF16),
            dma((2,)),
            dma((2, nb)), dma((nb,)),
            dma((2, nb)), dma((nb,)),
            dma((n2,)), dma((n2,)),
            dma((nw,)), dma((nw,)),
            dma((2,)), dma((2,)),
            dma((2, n2)), dma((2, n2)),
            dma((2, chunks)), dma((2, chunks)),
        ],
        compiler_params=pltpu.CompilerParams(
            collective_id=0, has_side_effects=True, vmem_limit_bytes=60 * 1024 * 1024
        ),
    )(
        audio, video, owner.reshape(1, rows), lengths.reshape(1, slots), clip_feats, proj_weight
    )


def solution(mesh):
    return jax.shard_map(
        functools.partial(shards, mesh.shape["wide"], mesh.shape["blk"]),
        mesh=mesh,
        in_specs=(
            P(("wide", "blk"), None),
            P(("wide", "blk"), None),
            P(("wide", "blk"), None),
            P(("wide", "blk"), None),
            P(("wide", "blk")),
            P(),
        ),
        out_specs=(P(("wide", "blk"), None), P(("wide", "blk"), None), P("wide", None)),
        check_vma=False,
    )
```

time: 168 us -> 79.5 us (0.47)
  waiting for transfers between devices: 131 us -> 0 us
  Pallas kernels: 0 us -> 73.1 us
  matrix products: 14.2 us -> 0 us
  between operations: 13.9 us -> 0.64 us
  local copies, waits for them, and re-layouts: 0.82 us -> 5.42 us
  other arithmetic: 4.2 us -> 0 us
  starting transfers between devices: 3.81 us -> 0 us
    pallas_call x0 -> x1, Pallas kernels: none -> 73.1 us  [shards(): pl.pallas_call(functools.partial(kernel, nw, nb), out_shape=(jax.ShapeDty...]
    all_gather x2 -> x0, waiting for transfers between devices: 43.3 us -> none  [the longest x1 30 us: shards(): gathered = lax.all_gather(audio, 'blk', axis=0, tiled=True)]
    reduce_scatter x1 -> x0, waiting for transfers between devices: 40.8 us -> none  [shards(): lax.psum_scatter(cols_dot(pooled, pre_grad).astype(jnp.bfloat16), 'wide',...]
    psum x1 -> x0, waiting for transfers between devices: 36.2 us -> none  [shards(): weight_grad = lax.psum(partial_rows, 'blk').astype(jnp.float32)]
    dot_general x6 -> x0, matrix products: 14.2 us -> none  [the longest x1 4.22 us: shards(): preact = jnp.dot(pooled, proj_weight, preferred_element_type=jnp.float32)]
    all_to_all x1 -> x0, waiting for transfers between devices: 8.88 us -> none  [shards(): lax.all_to_all(packed, 'wide', split_axis=0, concat_axis=0, tiled=True)]
    unnamed x14 -> x3, local copies, waits for them, and re-layouts: 0.82 us -> 5.42 us
    all_to_all x1 -> x0, starting transfers between devices: 3.65 us -> none  [shards(): lax.all_to_all(packed, 'wide', split_axis=0, concat_axis=0, tiled=True)]
  transfers between devices with their start and end apart: 5 -> 0, of which waited for: 5 -> 0; matrix products, arithmetic and copies ran while one was open for 8% -> 0% of each run, Pallas kernels for 0% -> 0%
where the time goes in v1:
time: 79.5 us; the launch traced here: 79.2 us
  Pallas kernels  73.1 us (92%)
  local copies, waits for them, and re-layouts  5.42 us (7%)
    pallas_call x1, Pallas kernels, shards(): pl.pallas_call(functools.partial(kernel, nw, nb), out_shape=(jax.ShapeDty...  73.1 us
    unnamed x3, local copies, waits for them, and re-layouts  5.42 us

profile of v1, /device:TPU:0, one launch (start us, length us, event | category | flops | bytes accessed | tf_op | source)
XLA Modules:
  0.0 79.2 jit_solution(17141620457483764754)
XLA Ops:
  0.6 73.1 %shard_map.85 = (bf16[128,1024]{1,0:T(8,128)(2,1)}, bf16[256,1024]{1,0:T(8,128)(2,1)}, f32[128,1024]{1,0:T(8,128)}) custom-call(bf16[128,1024]{1,0:T(8,128)(2,1)} %audio.1, bf16[128,1024]{1,0:T(8,128)(2,1)} %video.1, s32[1,128]{1,0:T(1,128)} %bitcast.3, s32[1,256]{1,0:T(1,128)} %bitcast.2, bf16[256,1024]{1,0:T(8,128)(2,1)} %feats_hbm.1, ...), custom_call_target="tpu_custom_call" | custom-call | tf_op jit(solution)/shard_map/pallas_call | solution.py:391
  73.8 1.7 %copy.12 = bf16[128,1024]{1,0:T(8,128)(2,1)} copy(bf16[128,1024]{1,0:T(8,128)(2,1)} %get-tuple-element.6) | data formatting | bytes 524288
  75.4 1.9 %copy.13 = bf16[256,1024]{1,0:T(8,128)(2,1)} copy(bf16[256,1024]{1,0:T(8,128)(2,1)} %get-tuple-element.7) | data formatting | bytes 1048576
  77.3 1.9 %copy.14 = f32[128,1024]{1,0:T(8,128)} copy(f32[128,1024]{1,0:T(8,128)} %get-tuple-element.8) | data formatting | bytes 1048576

commit v2 on v1

--- a/solution.py
+++ b/solution.py
@@ -10,7 +10,7 @@
 F32 = jnp.float32
 BF16 = jnp.bfloat16
 TILE = 256
-SPLIT = 2
+SPLIT = 4
 
 
 def dot(a, b):
@@ -194,41 +194,44 @@
     placing = (
         (lax.broadcasted_iota(jnp.int32, (slots, rows), 0) == target).astype(F32).astype(BF16)
     )
-    for t in range(width // TILE):
-        cols = slice(t * TILE, (t + 1) * TILE)
-        placed = dot(placing, v_grad[:, cols])
-        packed[:, :, cols] = placed.reshape(nw, cap, TILE).astype(BF16)
-
-    def exchange(peer):
+    def exchange(h, peer):
         return remote(
-            packed.at[peer], received.at[w], x_send.at[peer], x_recv.at[w], peer, k
-        )
-
-    @pl.loop(1, nw)
-    def _(d):
-        exchange(peer_of(d)).start()
-
-    received[w] = packed[w]
-
-    relay(1, v_buf, v_send, v_recv, audio, a_acc)
-
-    @pl.loop(1, nw)
-    def _(d):
-        peer = peer_of(d)
-        remote(
-            packed.at[peer], received.at[peer], x_send.at[peer], x_recv.at[peer], peer, k
-        ).wait_recv()
-
-    def grad_copy(h):
-        return remote(pre.at[h], pre_p.at[h], g_send.at[h], g_recv.at[h], partner, k)
+            packed.at[h, peer], received.at[h, w], x_send.at[h, peer], x_recv.at[h, w], peer, k
+        )
 
     for h in range(2):
         for t in range(half // TILE):
             lo = h * half + t * TILE
-            cols = slice(lo, lo + TILE)
-            grads = received[:, :, cols].astype(F32).reshape(slots, TILE)
-            pre[h, :, t * TILE : (t + 1) * TILE] = (grads * gate[:, cols]).astype(BF16)
+            placed = dot(placing, v_grad[:, lo : lo + TILE])
+            packed[h, :, :, t * TILE : (t + 1) * TILE] = placed.reshape(nw, cap, TILE).astype(BF16)
+
+        @pl.loop(1, nw)
+        def _(d):
+            exchange(h, peer_of(d)).start()
+
+        received[h, w] = packed[h, w]
+
+    def grad_copy(h):
+        return remote(pre.at[h], pre_p.at[h], g_send.at[h], g_recv.at[h], partner, k)
+
+    for h in range(2):
+
+        @pl.loop(1, nw)
+        def _(d):
+            peer = peer_of(d)
+            remote(
+                packed.at[h, peer], received.at[h, peer], x_send.at[h, peer],
+                x_recv.at[h, peer], peer, k,
+            ).wait_recv()
+
+        for t in range(half // TILE):
+            lo = h * half + t * TILE
+            part = slice(t * TILE, (t + 1) * TILE)
+            grads = received[h, :, :, part].astype(F32).reshape(slots, TILE)
+            pre[h, :, part] = (grads * gate[:, lo : lo + TILE]).astype(BF16)
         grad_copy(h).start()
+        if h == 0:
+            relay(1, v_buf, v_send, v_recv, audio, a_acc)
 
     @pl.loop(0, n2)
     def _(i):
@@ -289,6 +292,37 @@
         out = rows_dot(pre[0], weight[cols, :half]) + rows_dot(pre[1], weight[cols, half:])
         feats_out[:, cols] = (out * scale[...]).astype(BF16)
 
+    def sum_copy(side, q):
+        return remote(
+            zs.at[side, q], zr.at[side, q], z_send.at[side, q], z_recv.at[side, q],
+            w, k + 1 - 2 * side,
+        )
+
+    def scan(first, last):
+        @pl.loop(first, last)
+        def _(time):
+            for side in range(2):
+                place = k if side == 0 else nb - 1 - k
+                q = time - place
+
+                @pl.when((q >= 0) & (q < chunks))
+                def _():
+                    @pl.when(place > 0)
+                    def _():
+                        sum_copy(side, q).wait_recv()
+
+                    @pl.when(place < nb - 1)
+                    def _():
+                        @pl.when(place > 0)
+                        def _():
+                            zs[side, q] = (fin[q] + zr[side, q].astype(F32)).astype(BF16)
+
+                        @pl.when(place == 0)
+                        def _():
+                            zs[side, q] = fin[q].astype(BF16)
+
+                        sum_copy(side, q).start()
+
     for t in range(bits):
         for h in range(2):
             for combo in combos(t):
@@ -300,40 +334,16 @@
                     i = index(h, t + 1, 1, combo)
                     snd[h, slot_of(t + 1, combo)] = acc[h, i].astype(BF16)
                     scatter_copy(h, t + 1, combo).start()
-
-    for h in range(2):
-        for q in range(per_half):
-            fin[h * per_half + q] = acc[h, mine, :, q * chunk : (q + 1) * chunk]
-
-    def sum_copy(side, q):
-        return remote(
-            zs.at[side, q], zr.at[side, q], z_send.at[side, q], z_recv.at[side, q],
-            w, k + 1 - 2 * side,
-        )
-
-    @pl.loop(0, nb - 1 + chunks)
-    def _(time):
-        for side in range(2):
-            place = k if side == 0 else nb - 1 - k
-            q = time - place
-
-            @pl.when((q >= 0) & (q < chunks))
-            def _():
-                @pl.when(place > 0)
-                def _():
-                    sum_copy(side, q).wait_recv()
-
-                @pl.when(place < nb - 1)
-                def _():
-                    @pl.when(place > 0)
-                    def _():
-                        zs[side, q] = (fin[q] + zr[side, q].astype(F32)).astype(BF16)
-
-                    @pl.when(place == 0)
-                    def _():
-                        zs[side, q] = fin[q].astype(BF16)
-
-                    sum_copy(side, q).start()
+            else:
+                for q in range(per_half):
+                    fin[h * per_half + q] = acc[h, mine, :, q * chunk : (q + 1) * chunk]
+                if h == 0:
+                    scan(0, per_half)
+        if t == 0:
+            for s in range(max(2, nb - 1), nb):
+                relay(s, v_buf, v_send, v_recv, audio, a_acc)
+            audio_out[...] = a_acc[...].astype(BF16)
+    scan(per_half, nb - 1 + chunks)
 
     for q in range(chunks):
         cols = slice(q * chunk, (q + 1) * chunk)
@@ -347,10 +357,6 @@
         def _():
             weight_out[:, cols] += zr[1, q].astype(F32)
 
-    for s in range(max(2, nb - 1), nb):
-        relay(s, v_buf, v_send, v_recv, audio, a_acc)
-    audio_out[...] = a_acc[...].astype(BF16)
-
     finish(audio, a_buf, a_send, a_recv)
     finish(video, v_buf, v_send, v_recv)
 
@@ -360,7 +366,8 @@
 
     @pl.loop(1, nw)
     def _(d):
-        exchange(peer_of(d)).wait_send()
+        for h in range(2):
+            exchange(h, peer_of(d)).wait_send()
 
     for h in range(2):
         grad_copy(h).wait_send()
@@ -377,6 +384,15 @@
         @pl.when(k > 0)
         def _():
             sum_copy(1, q).wait_send()
+
+
+def store(*refs):
+    sems = refs[6]
+    copies = [pltpu.make_async_copy(refs[i], refs[3 + i], sems.at[i]) for i in range(3)]
+    for copy in copies:
+        copy.start()
+    for copy in copies:
+        copy.wait()
 
 
 def shards(nw, nb, audio, video, owner, clip_feats, lengths, proj_weight):
@@ -388,12 +404,12 @@
     vmem = pl.BlockSpec(memory_space=pltpu.VMEM)
     hbm = pl.BlockSpec(memory_space=pl.ANY)
     dma = pltpu.SemaphoreType.DMA
-    return pl.pallas_call(
+    outs = pl.pallas_call(
         functools.partial(kernel, nw, nb),
         out_shape=(
-            jax.ShapeDtypeStruct((rows, width), BF16),
-            jax.ShapeDtypeStruct((slots, width), BF16),
-            jax.ShapeDtypeStruct((block, width), F32),
+            pltpu.VMEM((rows, width), BF16),
+            pltpu.VMEM((slots, width), BF16),
+            pltpu.VMEM((block, width), F32),
         ),
         in_specs=[vmem, vmem, vmem, vmem, hbm, hbm],
         out_specs=(vmem, vmem, vmem),
@@ -410,8 +426,8 @@
             pltpu.VMEM((width, slots), BF16),
             pltpu.VMEM((n2, block, slots), BF16),
             pltpu.VMEM((slots, width), F32),
-            pltpu.VMEM((nw, cap, width), BF16),
-            pltpu.VMEM((nw, cap, width), BF16),
+            pltpu.VMEM((2, nw, cap, half), BF16),
+            pltpu.VMEM((2, nw, cap, half), BF16),
             pltpu.VMEM((2, slots, half), BF16),
             pltpu.VMEM((2, slots, half), BF16),
             pltpu.VMEM((2, n2, block, half), F32),
@@ -424,7 +440,7 @@
             dma((2, nb)), dma((nb,)),
             dma((2, nb)), dma((nb,)),
             dma((n2,)), dma((n2,)),
-            dma((nw,)), dma((nw,)),
+            dma((2, nw)), dma((2, nw)),
             dma((2,)), dma((2,)),
             dma((2, n2)), dma((2, n2)),
             dma((2, chunks)), dma((2, chunks)),
@@ -435,6 +451,13 @@
     )(
         audio, video, owner.reshape(1, rows), lengths.reshape(1, slots), clip_feats, proj_weight
     )
+    return pl.pallas_call(
+        store,
+        out_shape=tuple(jax.ShapeDtypeStruct(out.shape, out.dtype) for out in outs),
+        in_specs=[vmem, vmem, vmem],
+        out_specs=(hbm, hbm, hbm),
+        scratch_shapes=[dma((3,))],
+    )(*[pltpu.with_memory_space_constraint(out, pltpu.VMEM) for out in outs])
 
 
 def solution(mesh):

time: 79.5 us -> 76.4 us (0.961)
  local copies, waits for them, and re-layouts: 5.42 us -> 0 us
  Pallas kernels: 73.1 us -> 75.6 us
    unnamed x3 -> x0, local copies, waits for them, and re-layouts: 5.42 us -> none
    pallas_call x1 -> x2, Pallas kernels: 73.1 us -> 75.6 us  [the longest x1 74.5 us: shards(): pl.pallas_call(functools.partial(kernel, nw, nb), out_shape=(pltpu.VMEM((...]
where the time goes in v2:
time: 76.4 us; the launch traced here: 76.2 us
  Pallas kernels  75.6 us (99%)
    pallas_call x1, Pallas kernels, shards(): pl.pallas_call(functools.partial(kernel, nw, nb), out_shape=(pltpu.VMEM((...  74.5 us

profile of v2, /device:TPU:0, one launch (start us, length us, event | category | flops | bytes accessed | tf_op | source)
XLA Modules:
  0.0 76.2 jit_solution(10313362249391842380)
XLA Ops:
  0.6 74.5 %shard_map.85 = (bf16[128,1024]{1,0:T(8,128)(2,1)S(1)}, bf16[256,1024]{1,0:T(8,128)(2,1)S(1)}, f32[128,1024]{1,0:T(8,128)S(1)}) custom-call(bf16[128,1024]{1,0:T(8,128)(2,1)} %audio.1, bf16[128,1024]{1,0:T(8,128)(2,1)} %video.1, s32[1,128]{1,0:T(1,128)} %bitcast.3, s32[1,256]{1,0:T(1,128)} %bitcast.2, bf16[256,1024]{1,0:T(8,128)(2,1)} %feats_hbm.1, ...), custom_call_target="tpu_custom_call" | custom-call | tf_op jit(solution)/shard_map/pallas_call | solution.py:407
  75.1 1.1 %shard_map.86 = (bf16[128,1024]{1,0:T(8,128)(2,1)}, bf16[256,1024]{1,0:T(8,128)(2,1)}, f32[128,1024]{1,0:T(8,128)}) custom-call(bf16[128,1024]{1,0:T(8,128)(2,1)S(1)} %get-tuple-element.6.refs_0_, bf16[256,1024]{1,0:T(8,128)(2,1)S(1)} %get-tuple-element.7.refs_1_, f32[128,1024]{1,0:T(8,128)S(1)} %get-tuple-element.8.refs_2_), custom_call_target="tpu_custom_call" | custom-call | tf_op jit(solution)/shard_map/pallas_call | solution.py:454
